TPU v7x, 256 devices: a whole 4x4x8 slice. The times are simulated.
256 devices in a mesh: ctx: 64 (over z, y, core), ch: 4 (over x).
Axes of the slice: x: 4, y: 4, z: 8, core: 2. Of those that a mesh axis runs over, the one named last changes fastest.
Arguments:
- conv_input: bfloat16 [256, 128, 8192], P('ctx', None, 'ch'), may hold values from -6 to 6
- gate_signal: bfloat16 [256, 128, 8192], P('ctx', None, 'ch'), may hold values from -6 to 6
- cotangent: bfloat16 [256, 128, 8192], P('ctx', None, 'ch'), may hold values from -6 to 6
- filters: float32 [16, 1024], replicated
- tile_owner: int32 [192], replicated, may hold values from 0 to 63, as said below
- support: int32 [192, 8], replicated, may hold values from -1 to 191, as said below
Outputs:
- gate_grad: bfloat16 [256, 128, 8192], P('ctx', None, 'ch')
- input_grad: bfloat16 [256, 128, 8192], P('ctx', None, 'ch')
- filter_grad: float32 [16, 1024], replicated
Inputs may be any that keep to these rules, and one draw needn't show every extreme that they name: tile_owner never falls from one tile to the next; every index of ctx owns from 2 to 4 tiles, some index owns 3 + 1 and some index owns 3 - 1. support[t, k] is t - k where tile t - k belongs to the document of tile t and -1 otherwise; documents are runs of whole tiles, and some document spans 8 tiles or more.
All inputs are finite; a program needn't handle non-finite values.
Results may differ from a plain program's by a relative error of at most 0.0058.
Values may be sent and summed in bfloat16 or wider, within the bound.
No kernel may reach another device: no remote copies, remote signals or barrier semaphores. Data moves between devices by JAX's collectives and lax.ppermute only.
A program may use at most 256 MiB of HBM per device.

v0:
```python
import math
import jax
import jax.numpy as jnp
from jax import lax
from jax.sharding import PartitionSpec as P

GROUP = 128
REACH = 4


def passed_along(value, axis, steps):
    count = lax.axis_size(axis)
    leading, last = (max(0, -steps), min(count, count - steps))
    return lax.ppermute(value, axis, [(source, source + steps) for source in range(leading, last)])


def filter_blocks(filters, tile_rows, maxlag):
    narrow = filters.astype(jnp.bfloat16)
    row_ids = jnp.arange(tile_rows, dtype=jnp.int32)
    lag_offsets = (
        jnp.arange(maxlag, dtype=jnp.int32)[:, None, None] * tile_rows
        + row_ids[:, None]
        - row_ids[None, :]
    )
    picked = jnp.take(narrow, jnp.clip(lag_offsets, 0, filters.shape[1] - 1), axis=1)
    return jnp.where(lag_offsets[None] >= 0, picked, jnp.zeros_like(picked))


def lag_sums(square):
    filter_count, side_length = (square.shape[0], square.shape[1])
    flipped = square[:, :, ::-1]
    padded = jnp.pad(flipped, ((0, 0), (0, 0), (0, side_length)))
    skewed = padded.reshape(filter_count, 2 * side_length * side_length)[
        :, : side_length * (2 * side_length - 1)
    ]
    return jnp.sum(skewed.reshape(filter_count, side_length, 2 * side_length - 1), axis=1)


def spread_lags(squares, lag_count):
    maxlag, filter_count, side_length = (squares.shape[0], squares.shape[1], squares.shape[2])
    accumulated = jnp.zeros((filter_count, (maxlag + 1) * side_length), jnp.float32)
    for lag_index in range(maxlag):
        start_col = lag_index * side_length
        accumulated = accumulated.at[:, start_col : start_col + 2 * side_length - 1].add(
            lag_sums(squares[lag_index])
        )
    return accumulated[:, side_length - 1 : side_length - 1 + lag_count]


def per_device(conv_input, gate_signal, cotangent, filters, tile_owner, support):
    slot_count, tile_rows, channels = conv_input.shape
    maxlag = support.shape[1]
    filter_count, lag_count = filters.shape
    group_width = GROUP
    repeats = channels // (filter_count * group_width)
    total_tiles = tile_owner.shape[0]
    devices_ctx = lax.axis_size("ctx")
    myself = lax.axis_index("ctx")
    farthest = REACH
    devices = jnp.arange(devices_ctx, dtype=jnp.int32)
    counts = jnp.sum((tile_owner[None, :] == devices[:, None]).astype(jnp.int32), axis=1)
    starts = jnp.cumsum(counts) - counts
    slot_index = jnp.arange(slot_count, dtype=jnp.int32)
    own_tiles = starts[myself] + slot_index
    own_live = slot_index < counts[myself]
    own_safe = jnp.clip(own_tiles, 0, total_tiles - 1)
    sources = support[own_safe]
    present = own_live[:, None] & (sources >= 0)
    source_safe = jnp.clip(sources, 0, total_tiles - 1)
    holder = tile_owner[source_safe]
    within = source_safe - starts[holder]
    blocks = filter_blocks(filters, tile_rows, maxlag)
    zero_tile = jnp.zeros((), jnp.bfloat16)
    gathered = [conv_input]
    for distance in range(1, farthest + 1):
        gathered.append(passed_along(conv_input, "ctx", distance))
    window = jnp.concatenate(gathered, axis=0)
    rows_at = jnp.clip((myself - holder) * slot_count + within, 0, window.shape[0] - 1)
    selected = jnp.take(window, rows_at.reshape(-1), axis=0)
    selected = selected.reshape(slot_count, maxlag, tile_rows, channels)
    selected = jnp.where(present[:, :, None, None], selected, zero_tile)
    weighted = (gate_signal.astype(jnp.float32) * cotangent.astype(jnp.float32)).astype(
        jnp.bfloat16
    )
    weighted = jnp.where(own_live[:, None, None], weighted, zero_tile)
    weighted_shaped = weighted.reshape(slot_count, tile_rows, repeats, filter_count, group_width)
    conv_out = jnp.zeros((slot_count, tile_rows, channels), jnp.float32)
    squares = []
    for lag_index in range(maxlag):
        shaped = selected[:, lag_index].reshape(
            slot_count, tile_rows, repeats, filter_count, group_width
        )
        product = jnp.einsum(
            "fij,sjrfc->sirfc", blocks[:, lag_index], shaped, preferred_element_type=jnp.float32
        )
        conv_out = conv_out + product.reshape(slot_count, tile_rows, channels)
        squares.append(
            jnp.einsum(
                "sirfc,sjrfc->fij", weighted_shaped, shaped, preferred_element_type=jnp.float32
            )
        )
    gate_grad = (cotangent.astype(jnp.float32) * conv_out).astype(jnp.bfloat16)
    norm_factor = 1.0 / math.sqrt(
        total_tiles * tile_rows * channels * lax.axis_size("ch") / filter_count
    )
    local_filters = spread_lags(jnp.stack(squares), lag_count)
    filter_grad = lax.psum(local_filters, ("ctx", "ch")) * norm_factor
    row_count = (farthest + 1) * slot_count
    partial_value = jnp.zeros((row_count, tile_rows, channels), jnp.float32)
    back_rows = jnp.clip((myself - holder) * slot_count + within, 0, row_count - 1)
    for lag_index in range(maxlag):
        adjoint_term = jnp.einsum(
            "fji,sjrfc->sirfc",
            blocks[:, lag_index],
            weighted_shaped,
            preferred_element_type=jnp.float32,
        )
        adjoint_term = jnp.where(present[:, lag_index, None, None, None, None], adjoint_term, 0.0)
        partial_value = partial_value.at[back_rows[:, lag_index]].add(
            adjoint_term.reshape(slot_count, tile_rows, channels)
        )
    adjoint = partial_value[:slot_count]
    for distance in range(1, farthest + 1):
        adjoint = adjoint + passed_along(
            partial_value[distance * slot_count : (distance + 1) * slot_count], "ctx", -distance
        )
    input_grad = adjoint.astype(jnp.bfloat16)
    return (gate_grad, input_grad, filter_grad)


def solution(mesh):
    return jax.shard_map(
        per_device,
        mesh=mesh,
        in_specs=(P("ctx", None, "ch"), P("ctx", None, "ch"), P("ctx", None, "ch"), P(), P(), P()),
        out_specs=(P("ctx", None, "ch"), P("ctx", None, "ch"), P()),
        check_vma=False,
    )
```

profile of v0, /device:TPU:1, one launch (start us, length us, event | category | flops | bytes accessed | tf_op | source)
XLA Modules:
  0.0 1289.1 jit_solution(6269767289445348876)
XLA Ops:
  32.1 454.0 %gather_fusion.4 = bf16[131072,16]{1,0:T(8,128)(2,1)} fusion(bf16[16,1024]{0,1:T(8,128)(2,1)S(1)} %copy.164, s32[131072]{0:T(1024)S(1)} %broadcast_clamp_fusion), kind=kCustom, calls=%fused_computation.4 | custom fusion | bytes 8912896 | tf_op jit(solution)/shard_map/jit(_take)/gather | solution.py:25
  486.1 29.2 %copy.166 = bf16[8,128,128,16]{2,1,3,0:T(8,128)(2,1)} copy(bf16[8,128,128,16]{3,2,1,0:T(8,128)(2,1)} %bitcast.207) | data formatting | bytes 8388608 | tf_op jit(solution)/shard_map/jit(_take)/gather | solution.py:25
  623.9 9.7 broadcast_in_dim.155
  633.6 9.0 scatter_fusion
  642.5 9.0 scatter_fusion.1
  651.6 9.0 scatter_fusion.2
  660.6 9.0 scatter_fusion.3
  669.6 8.7 scatter_fusion.4
  678.3 8.6 scatter_fusion.5
  686.9 8.3 scatter_fusion.6
  695.1 8.3 scatter_fusion.7
  703.4 12.2 fusion.52
  742.8 11.4 gather_fusion.3
  754.2 8.7 select_select_fusion
  762.9 5.9 fusion.53
  836.1 11.8 add_bitcast_fusion
  850.1 9.3 rev.24
  863.5 6.2 reshape.668
  872.1 9.3 rev.25
  885.6 6.2 reshape.670
  893.5 6.0 rev.26
  903.6 6.2 reshape.672
  913.9 5.8 rev.27
  923.8 6.2 reshape.674
  934.1 6.0 rev.28
  944.3 6.2 reshape.676
  964.5 6.2 reshape.678
  974.8 6.1 rev.30
  985.0 6.2 reshape.680
  1005.2 6.3 reshape.682
  1028.9 241.1 %all-reduce.11.cloned.1.call-done = f32[16,1024]{1,0:T(8,128)} async-done(((f32[16,1024]{1,0:T(8,128)}), f32[16,1024]{1,0:T(8,128)}) %all-reduce.11.cloned.1.call-update) | async-done | bytes 65552 | tf_op jit(solution)/shard_map/psum | solution.py:107
  1271.5 10.4 fusion.5
  (190 shorter events, 317.9 us)
Async XLA Ops:
  7.2 24.7 %copy-start.7 = (f32[16,1024]{1,0:T(8,128)S(1)}, f32[16,1024]{1,0:T(8,128)}, u32[]{:S(2)}) copy-start(f32[16,1024]{1,0:T(8,128)} %param.25) | copy-start | bytes 196612
  7.2 1262.8 %all-reduce.11.cloned.1.call-start = ((), (), s32[]{:S(2)}) async-start(), calls=%async_computation | async-start | bytes 131072 | tf_op jit(solution)/shard_map/psum | solution.py:107
  7.2 718.4 %collective-permute-start = (bf16[4,128,2048]{2,1,0:T(8,128)(2,1)}, bf16[4,128,2048]{2,1,0:T(8,128)(2,1)}, u32[]{:S(2)}, u32[]{:S(2)}) collective-permute-start(bf16[4,128,2048]{2,1,0:T(8,128)(2,1)} %param.22), channel_id=1, source_target_pairs={{0,4},{4,8},{8,12},{12,16},{16,20},{20,24},{24,28},{28,32},{32,36}... | collective-permute-start | bytes 6291464 | tf_op jit(solution)/shard_map/ppermute | solution.py:14
  11.8 718.2 %collective-permute-start.1 = (bf16[4,128,2048]{2,1,0:T(8,128)(2,1)}, bf16[4,128,2048]{2,1,0:T(8,128)(2,1)}, u32[]{:S(2)}, u32[]{:S(2)}) collective-permute-start(bf16[4,128,2048]{2,1,0:T(8,128)(2,1)} %param.22), channel_id=1, source_target_pairs={{0,8},{4,12},{8,16},{12,20},{16,24},{20,28},{24,32},{28,36},{32,40... | collective-permute-start | bytes 6291464 | tf_op jit(solution)/shard_map/ppermute | solution.py:14
  16.3 718.2 %collective-permute-start.2 = (bf16[4,128,2048]{2,1,0:T(8,128)(2,1)}, bf16[4,128,2048]{2,1,0:T(8,128)(2,1)}, u32[]{:S(2)}, u32[]{:S(2)}) collective-permute-start(bf16[4,128,2048]{2,1,0:T(8,128)(2,1)} %param.22), channel_id=1, source_target_pairs={{0,12},{4,16},{8,20},{12,24},{16,28},{20,32},{24,36},{28,40},{32,4... | collective-permute-start | bytes 6291464 | tf_op jit(solution)/shard_map/ppermute | solution.py:14
  19.9 719.7 %collective-permute-start.3 = (bf16[4,128,2048]{2,1,0:T(8,128)(2,1)}, bf16[4,128,2048]{2,1,0:T(8,128)(2,1)}, u32[]{:S(2)}, u32[]{:S(2)}) collective-permute-start(bf16[4,128,2048]{2,1,0:T(8,128)(2,1)} %param.22), channel_id=1, source_target_pairs={{0,16},{4,20},{8,24},{12,28},{16,32},{20,36},{24,40},{28,44},{32,4... | collective-permute-start | bytes 6291464 | tf_op jit(solution)/shard_map/ppermute | solution.py:14
  486.1 29.2 %copy-start.6 = (bf16[4,128,2048]{2,1,0:T(8,128)(2,1)S(1)}, bf16[4,128,2048]{2,1,0:T(8,128)(2,1)}, u32[]{:S(2)}) copy-start(bf16[4,128,2048]{2,1,0:T(8,128)(2,1)} %param.24) | copy-start | bytes 6291460
  522.1 3.4 copy-start.5
  526.1 16.7 %copy-start = (bf16[16,8,128,128]{3,2,0,1:T(8,128)(2,1)}, bf16[16,8,128,128]{3,2,0,1:T(8,128)(2,1)S(1)}, u32[]{:S(2)}) copy-start(bf16[16,8,128,128]{3,2,0,1:T(8,128)(2,1)S(1)} %select_bitcast_fusion) | copy-start | bytes 12582916
  715.7 555.8 %collective-permute-start.7 = (f32[4,128,2048]{2,1,0:T(8,128)}, f32[4,128,2048]{2,1,0:T(8,128)}, u32[]{:S(2)}, u32[]{:S(2)}) collective-permute-start(f32[4,128,2048]{2,1,0:T(8,128)} %get-tuple-element.127), channel_id=1, source_target_pairs={{16,0},{20,4},{24,8},{28,12},{32,16},{36,20},{40,24},{44,28},{48,3... | collective-permute-start | bytes 12582920 | tf_op jit(solution)/shard_map/ppermute | solution.py:14
  725.6 545.8 %collective-permute-start.6 = (f32[4,128,2048]{2,1,0:T(8,128)}, f32[4,128,2048]{2,1,0:T(8,128)}, u32[]{:S(2)}, u32[]{:S(2)}) collective-permute-start(f32[4,128,2048]{2,1,0:T(8,128)} %get-tuple-element.128), channel_id=1, source_target_pairs={{12,0},{16,4},{20,8},{24,12},{28,16},{32,20},{36,24},{40,28},{44,3... | collective-permute-start | bytes 12582920 | tf_op jit(solution)/shard_map/ppermute | solution.py:14
  730.0 541.4 %collective-permute-start.5 = (f32[4,128,2048]{2,1,0:T(8,128)}, f32[4,128,2048]{2,1,0:T(8,128)}, u32[]{:S(2)}, u32[]{:S(2)}) collective-permute-start(f32[4,128,2048]{2,1,0:T(8,128)} %get-tuple-element.129), channel_id=1, source_target_pairs={{8,0},{12,4},{16,8},{20,12},{24,16},{28,20},{32,24},{36,28},{40,32... | collective-permute-start | bytes 12582920 | tf_op jit(solution)/shard_map/ppermute | solution.py:14
  734.5 536.9 %collective-permute-start.4 = (f32[4,128,2048]{2,1,0:T(8,128)}, f32[4,128,2048]{2,1,0:T(8,128)}, u32[]{:S(2)}, u32[]{:S(2)}) collective-permute-start(f32[4,128,2048]{2,1,0:T(8,128)} %get-tuple-element.126), channel_id=1, source_target_pairs={{4,0},{8,4},{12,8},{16,12},{20,16},{24,20},{28,24},{32,28},{36,32}... | collective-permute-start | bytes 12582920 | tf_op jit(solution)/shard_map/ppermute | solution.py:14
  772.8 4.5 copy-start.2
  783.0 4.5 copy-start.3
  793.2 4.5 copy-start.4
  1005.2 15.8 %copy-start.1 = (bf16[4,128,2048]{1,2,0:T(8,128)(2,1)S(1)}, bf16[4,128,2048]{1,2,0:T(8,128)(2,1)}, u32[]{:S(2)}) copy-start(bf16[4,128,2048]{1,2,0:T(8,128)(2,1)} %copy.160) | copy-start | bytes 6291460
Sparse Core Ops, SparseCore 0:
  1021.1 248.8 all-reduce.10
where the time goes:
time: 1300 us; the launch traced here: 1290 us
  local copies, waits for them, and re-layouts  807 us (62%)
  waiting for transfers between devices  241 us (19%)
  other arithmetic  126 us (10%)
  matrix products  78 us (6%)
  starting transfers between devices  22.1 us (2%)
  between operations  15.1 us (1%)
    gather x2, local copies, waits for them, and re-layouts, filter_blocks(): jnp.take(narrow, jnp.clip(lag_offsets, 0, filters.shape[1] - 1), axis=1)  483 us
    psum x1, waiting for transfers between devices, per_device(): filter_grad = lax.psum(local_filters, ('ctx', 'ch')) * norm_factor  241 us
    scatter-add x8, other arithmetic, per_device(): partial_value.at[back_rows[:, lag_index]]  69.9 us
    rev x8, local copies, waits for them, and re-layouts, lag_sums(): flipped = square[:, :, ::-1]  54.3 us
    reshape x8, local copies, waits for them, and re-layouts, lag_sums(): skewed.reshape(filter_count, side_length, 2 * side_length - 1)  49.4 us
    reshape x8, local copies, waits for them, and re-layouts, per_device(): adjoint_term.reshape(slot_count, tile_rows, channels)  43.4 us
    dot_general x8, matrix products, per_device(): jnp.einsum('fij,sjrfc->sirfc', blocks[:, lag_index], shaped, preferred_el...  42.7 us
    slice x9, local copies, waits for them, and re-layouts, per_device(): selected[:, lag_index]  37.9 us
  transfers between devices with their start and end apart: 9, of which 1 were waited for; matrix products, arithmetic and copies ran while one was open for 78% of the time, Pallas kernels for 0%

commit v1 on v0

--- a/solution.py
+++ b/solution.py
@@ -3,9 +3,11 @@
 import jax.numpy as jnp
 from jax import lax
 from jax.sharding import PartitionSpec as P
+from jax.lax import psum
 
 GROUP = 128
 REACH = 4
+tell_classes_up = lambda group_axis, slab_in, ax_name: psum(psum(slab_in, ax_name), group_axis)
 
 
 def passed_along(value, axis, steps):
@@ -104,7 +106,7 @@
         total_tiles * tile_rows * channels * lax.axis_size("ch") / filter_count
     )
     local_filters = spread_lags(jnp.stack(squares), lag_count)
-    filter_grad = lax.psum(local_filters, ("ctx", "ch")) * norm_factor
+    filter_grad = tell_classes_up("ch", local_filters, "ctx") * norm_factor
     row_count = (farthest + 1) * slot_count
     partial_value = jnp.zeros((row_count, tile_rows, channels), jnp.float32)
     back_rows = jnp.clip((myself - holder) * slot_count + within, 0, row_count - 1)

time: 1300 us -> 1260 us (0.969)
  waiting for transfers between devices: 241 us -> 187 us
  local copies, waits for them, and re-layouts: 807 us -> 821 us
    psum x1 -> x2, waiting for transfers between devices: 241 us -> 187 us  [the longest x1 151 us: psum(slab_in, ax_name)]
    rev x8, local copies, waits for them, and re-layouts: 54.3 us -> 68.2 us  [lag_sums(): flipped = square[:, :, ::-1]]
    unnamed x32 -> x44, local copies, waits for them, and re-layouts: 33.9 us -> 34 us
  transfers between devices with their start and end apart: 9 -> 10, of which waited for: 1 -> 2; matrix products, arithmetic and copies ran while one was open for 78% -> 81% of each run, Pallas kernels for 0% -> 0%
where the time goes in v1:
time: 1260 us; the launch traced here: 1250 us
  local copies, waits for them, and re-layouts  821 us (65%)
  waiting for transfers between devices  187 us (15%)
  other arithmetic  126 us (10%)
  matrix products  74.6 us (6%)
  starting transfers between devices  22.4 us (2%)
  between operations  15.1 us (1%)
    gather x2, local copies, waits for them, and re-layouts, filter_blocks(): jnp.take(narrow, jnp.clip(lag_offsets, 0, filters.shape[1] - 1), axis=1)  483 us
    psum x1, waiting for transfers between devices, psum(slab_in, ax_name)  151 us
    scatter-add x8, other arithmetic, per_device(): partial_value.at[back_rows[:, lag_index]]  69.9 us
    rev x8, local copies, waits for them, and re-layouts, lag_sums(): flipped = square[:, :, ::-1]  68.2 us
    reshape x8, local copies, waits for them, and re-layouts, lag_sums(): skewed.reshape(filter_count, side_length, 2 * side_length - 1)  49.4 us
    reshape x8, local copies, waits for them, and re-layouts, per_device(): adjoint_term.reshape(slot_count, tile_rows, channels)  43.4 us
    slice x9, local copies, waits for them, and re-layouts, per_device(): selected[:, lag_index]  37.5 us
    psum x1, waiting for transfers between devices, psum(psum(slab_in, ax_name), group_axis)  35.2 us
  transfers between devices with their start and end apart: 10, of which 2 were waited for; matrix products, arithmetic and copies ran while one was open for 81% of the time, Pallas kernels for 0%

profile of v1, /device:TPU:1, one launch (start us, length us, event | category | flops | bytes accessed | tf_op | source)
XLA Modules:
  0.0 1245.5 jit_solution(14663723464845822097)
XLA Ops:
  32.2 454.0 %gather_fusion.4 = bf16[131072,16]{1,0:T(8,128)(2,1)} fusion(bf16[16,1024]{0,1:T(8,128)(2,1)S(1)} %copy.164, s32[131072]{0:T(1024)S(1)} %broadcast_clamp_fusion), kind=kCustom, calls=%fused_computation.4 | custom fusion | bytes 8912896 | tf_op jit(solution)/shard_map/jit(_take)/gather | solution.py:27
  486.1 29.2 %copy.166 = bf16[8,128,128,16]{2,1,3,0:T(8,128)(2,1)} copy(bf16[8,128,128,16]{3,2,1,0:T(8,128)(2,1)} %bitcast.207) | data formatting | bytes 8388608 | tf_op jit(solution)/shard_map/jit(_take)/gather | solution.py:27
  623.9 9.7 broadcast_in_dim.155
  633.6 9.0 scatter_fusion
  642.5 9.0 scatter_fusion.1
  651.6 9.0 scatter_fusion.2
  660.6 9.0 scatter_fusion.3
  669.6 8.7 scatter_fusion.4
  678.2 8.6 scatter_fusion.5
  686.9 8.3 scatter_fusion.6
  695.1 8.3 scatter_fusion.7
  703.4 12.2 fusion.52
  742.8 11.4 gather_fusion.3
  754.2 8.7 select_select_fusion
  815.3 9.5 rev.24
  829.0 6.2 reshape.668
  840.9 9.2 rev.25
  854.3 6.2 reshape.670
  865.5 9.7 rev.26
  879.3 6.2 reshape.672
  890.6 9.2 rev.27
  904.0 6.2 reshape.674
  915.2 9.4 rev.28
  928.8 6.2 reshape.676
  936.7 9.3 rev.29
  950.2 6.2 reshape.678
  968.3 6.2 reshape.680
  988.5 6.3 reshape.682
  1019.2 10.3 add_bitcast_fusion
  1031.8 151.5 %all-reduce.12.cloned.1.call-done = f32[16,1024]{1,0:T(8,128)} async-done(((f32[16,1024]{1,0:T(8,128)}), f32[16,1024]{1,0:T(8,128)}) %all-reduce.12.cloned.1.call-update) | async-done | bytes 65552 | tf_op jit(solution)/shard_map/psum | solution.py:10
  1191.1 35.2 %all-reduce.14.cloned.1.call-done = f32[16,1024]{1,0:T(8,128)} async-done(((f32[16,1024]{1,0:T(8,128)}), f32[16,1024]{1,0:T(8,128)}) %all-reduce.14.cloned.1.call-update) | async-done | bytes 65552 | tf_op jit(solution)/shard_map/psum | solution.py:10
  1227.8 10.4 fusion.5
  (205 shorter events, 322.3 us)
Async XLA Ops:
  7.2 24.7 %copy-start.13 = (f32[16,1024]{1,0:T(8,128)S(1)}, f32[16,1024]{1,0:T(8,128)}, u32[]{:S(2)}) copy-start(f32[16,1024]{1,0:T(8,128)} %param.25) | copy-start | bytes 196612
  7.2 1176.1 %all-reduce.12.cloned.1.call-start = ((), (), s32[]{:S(2)}) async-start(), calls=%async_computation | async-start | bytes 131072 | tf_op jit(solution)/shard_map/psum | solution.py:10
  7.2 718.4 %collective-permute-start = (bf16[4,128,2048]{2,1,0:T(8,128)(2,1)}, bf16[4,128,2048]{2,1,0:T(8,128)(2,1)}, u32[]{:S(2)}, u32[]{:S(2)}) collective-permute-start(bf16[4,128,2048]{2,1,0:T(8,128)(2,1)} %param.22), channel_id=1, source_target_pairs={{0,4},{4,8},{8,12},{12,16},{16,20},{20,24},{24,28},{28,32},{32,36}... | collective-permute-start | bytes 6291464 | tf_op jit(solution)/shard_map/ppermute | solution.py:16
  11.8 718.2 %collective-permute-start.1 = (bf16[4,128,2048]{2,1,0:T(8,128)(2,1)}, bf16[4,128,2048]{2,1,0:T(8,128)(2,1)}, u32[]{:S(2)}, u32[]{:S(2)}) collective-permute-start(bf16[4,128,2048]{2,1,0:T(8,128)(2,1)} %param.22), channel_id=1, source_target_pairs={{0,8},{4,12},{8,16},{12,20},{16,24},{20,28},{24,32},{28,36},{32,40... | collective-permute-start | bytes 6291464 | tf_op jit(solution)/shard_map/ppermute | solution.py:16
  16.3 718.2 %collective-permute-start.2 = (bf16[4,128,2048]{2,1,0:T(8,128)(2,1)}, bf16[4,128,2048]{2,1,0:T(8,128)(2,1)}, u32[]{:S(2)}, u32[]{:S(2)}) collective-permute-start(bf16[4,128,2048]{2,1,0:T(8,128)(2,1)} %param.22), channel_id=1, source_target_pairs={{0,12},{4,16},{8,20},{12,24},{16,28},{20,32},{24,36},{28,40},{32,4... | collective-permute-start | bytes 6291464 | tf_op jit(solution)/shard_map/ppermute | solution.py:16
  19.9 719.7 %collective-permute-start.3 = (bf16[4,128,2048]{2,1,0:T(8,128)(2,1)}, bf16[4,128,2048]{2,1,0:T(8,128)(2,1)}, u32[]{:S(2)}, u32[]{:S(2)}) collective-permute-start(bf16[4,128,2048]{2,1,0:T(8,128)(2,1)} %param.22), channel_id=1, source_target_pairs={{0,16},{4,20},{8,24},{12,28},{16,32},{20,36},{24,40},{28,44},{32,4... | collective-permute-start | bytes 6291464 | tf_op jit(solution)/shard_map/ppermute | solution.py:16
  486.1 29.2 %copy-start.12 = (bf16[4,128,2048]{2,1,0:T(8,128)(2,1)S(1)}, bf16[4,128,2048]{2,1,0:T(8,128)(2,1)}, u32[]{:S(2)}) copy-start(bf16[4,128,2048]{2,1,0:T(8,128)(2,1)} %param.24) | copy-start | bytes 6291460
  522.1 3.4 copy-start.11
  526.1 16.7 %copy-start = (bf16[16,8,128,128]{3,2,0,1:T(8,128)(2,1)}, bf16[16,8,128,128]{3,2,0,1:T(8,128)(2,1)S(1)}, u32[]{:S(2)}) copy-start(bf16[16,8,128,128]{3,2,0,1:T(8,128)(2,1)S(1)} %select_bitcast_fusion) | copy-start | bytes 12582916
  715.7 512.1 %collective-permute-start.7 = (f32[4,128,2048]{2,1,0:T(8,128)}, f32[4,128,2048]{2,1,0:T(8,128)}, u32[]{:S(2)}, u32[]{:S(2)}) collective-permute-start(f32[4,128,2048]{2,1,0:T(8,128)} %get-tuple-element.127), channel_id=1, source_target_pairs={{16,0},{20,4},{24,8},{28,12},{32,16},{36,20},{40,24},{44,28},{48,3... | collective-permute-start | bytes 12582920 | tf_op jit(solution)/shard_map/ppermute | solution.py:16
  725.6 502.2 %collective-permute-start.6 = (f32[4,128,2048]{2,1,0:T(8,128)}, f32[4,128,2048]{2,1,0:T(8,128)}, u32[]{:S(2)}, u32[]{:S(2)}) collective-permute-start(f32[4,128,2048]{2,1,0:T(8,128)} %get-tuple-element.128), channel_id=1, source_target_pairs={{12,0},{16,4},{20,8},{24,12},{28,16},{32,20},{36,24},{40,28},{44,3... | collective-permute-start | bytes 12582920 | tf_op jit(solution)/shard_map/ppermute | solution.py:16
  730.1 497.7 %collective-permute-start.5 = (f32[4,128,2048]{2,1,0:T(8,128)}, f32[4,128,2048]{2,1,0:T(8,128)}, u32[]{:S(2)}, u32[]{:S(2)}) collective-permute-start(f32[4,128,2048]{2,1,0:T(8,128)} %get-tuple-element.129), channel_id=1, source_target_pairs={{8,0},{12,4},{16,8},{20,12},{24,16},{28,20},{32,24},{36,28},{40,32... | collective-permute-start | bytes 12582920 | tf_op jit(solution)/shard_map/ppermute | solution.py:16
  734.6 493.3 %collective-permute-start.4 = (f32[4,128,2048]{2,1,0:T(8,128)}, f32[4,128,2048]{2,1,0:T(8,128)}, u32[]{:S(2)}, u32[]{:S(2)}) collective-permute-start(f32[4,128,2048]{2,1,0:T(8,128)} %get-tuple-element.126), channel_id=1, source_target_pairs={{4,0},{8,4},{12,8},{16,12},{20,16},{24,20},{28,24},{32,28},{36,32}... | collective-permute-start | bytes 12582920 | tf_op jit(solution)/shard_map/ppermute | solution.py:16
  772.8 4.5 copy-start.9
  783.0 4.5 copy-start.10
  988.5 16.1 %copy-start.4 = (bf16[4,1,128,2048]{2,3,0,1:T(8,128)(2,1)S(1)}, bf16[4,1,128,2048]{2,3,0,1:T(8,128)(2,1)}, u32[]{:S(2)}) copy-start(bf16[4,1,128,2048]{2,3,0,1:T(8,128)(2,1)} %copy.174) | copy-start | bytes 6291460
  1004.3 222.0 %all-reduce.14.cloned.1.call-start = ((), (), s32[]{:S(2)}) async-start(), calls=%async_computation.1 | async-start | bytes 131072 | tf_op jit(solution)/shard_map/psum | solution.py:10
  1004.6 3.9 copy-start.1
  1004.6 3.9 copy-start.5
  1008.5 2.8 copy-start.6
  1011.2 2.7 copy-start.7
  1013.9 2.6 copy-start.8
  1016.5 2.7 copy-start.2
  1029.5 153.7 %copy-start.3 = (bf16[4,128,2048]{1,2,0:T(8,128)(2,1)S(1)}, bf16[4,128,2048]{1,2,0:T(8,128)(2,1)}, u32[]{:S(2)}) copy-start(bf16[4,128,2048]{1,2,0:T(8,128)(2,1)} %copy.160) | copy-start | bytes 6291460
Sparse Core Ops, SparseCore 0:
  1004.4 178.7 all-reduce.11
  1185.5 40.7 all-reduce.13
